TPU v7x, 128 devices: a whole 4x4x4 slice. The times are simulated.
128 devices in a mesh: req: 4 (over z), exp: 32 (over x, y, core).
Axes of the slice: x: 4, y: 4, z: 4, core: 2. Of those that a mesh axis runs over, the one named last changes fastest.
Arguments:
- attn_out: bfloat16 [16384, 2048], P(('req', 'exp')), may hold values from -6 to 6
- residual: bfloat16 [16384, 2048], P(('req', 'exp')), may hold values from -6 to 6
- out_weight: bfloat16 [2048, 2048], P('exp'), may hold values from -0.125 to 0.125
- norm_gain: float32 [2048], replicated, may hold values from 0.25 to 1.75
- expert_ids: int32 [16384, 6], P(('req', 'exp')), may hold values from 0 to 31, all different within a row; in each aligned block of 128 rows (0 to 127, 128 to 255, ...) at most 36 rows name the same one
- gate_weights: float32 [16384, 6], P(('req', 'exp')), may hold values from 0.05 to 0.5
- expert_gate: bfloat16 [32, 2048, 1408], P('exp'), may hold values from -0.125 to 0.125
- expert_up: bfloat16 [32, 2048, 1408], P('exp'), may hold values from -0.125 to 0.125
- expert_down: bfloat16 [32, 1408, 2048], P('exp'), may hold values from -0.15625 to 0.15625
- shared_gate: bfloat16 [2048, 1408], P(None, 'req'), may hold values from -0.125 to 0.125
- shared_up: bfloat16 [2048, 1408], P(None, 'req'), may hold values from -0.125 to 0.125
- shared_down: bfloat16 [2048, 1408], P(None, 'req'), may hold values from -0.15625 to 0.15625
Outputs:
- mixed: bfloat16 [16384, 2048], P(('req', 'exp'))
Inputs may be any that keep to these rules, and one draw needn't show every extreme that they name: `expert_ids`: within the rows of one device no expert is named by more than 36 rows, and each row names 6 different experts.
All inputs are finite; a program needn't handle non-finite values.
Results may differ from a plain program's by a relative error of at most 0.012.
Values may be sent and summed in bfloat16 or wider, within the bound.
A program may use at most 192 MiB of HBM per device.

v0:
```python
import jax
import jax.numpy as jnp
from jax import lax
from jax.sharding import PartitionSpec as P


def body(
    attn_out,
    residual,
    out_weight,
    norm_gain,
    expert_ids,
    gate_weights,
    expert_gate,
    expert_up,
    expert_down,
    shared_gate,
    shared_up,
    shared_down,
):
    row_count, width = attn_out.shape
    topk = expert_ids.shape[1]
    experts = lax.axis_size("exp")
    capacity = min(row_count, 3 * row_count * topk // (2 * experts))
    req = lax.axis_size("req")
    quarter = out_weight.shape[0] // req
    piece = lax.dynamic_slice_in_dim(out_weight, lax.axis_index("req") * quarter, quarter, 0)
    proj = jnp.dot(
        attn_out,
        lax.all_gather(piece, ("exp", "req"), axis=0, tiled=True),
        preferred_element_type=jnp.float32,
    )
    stream = (residual.astype(jnp.float32) + proj).astype(jnp.bfloat16)
    stream_f = stream.astype(jnp.float32)
    scale = lax.rsqrt(jnp.mean(stream_f * stream_f, axis=1, keepdims=True) + 1e-06)
    normed = (stream_f * scale * norm_gain).astype(jnp.bfloat16)
    flat_ids = expert_ids.reshape(-1)
    onehot = (flat_ids[:, None] == jnp.arange(experts, dtype=jnp.int32)[None, :]).astype(jnp.int32)
    position = jnp.sum(jnp.cumsum(onehot, axis=0) * onehot, axis=1) - 1
    slot = flat_ids * capacity + position
    source_row = jnp.arange(row_count * topk, dtype=jnp.int32) // topk
    table = jnp.full((experts * capacity,), row_count, jnp.int32).at[slot].set(source_row)
    rows = jnp.arange(row_count, dtype=jnp.int32)
    pick = (table.reshape(experts, capacity)[:, :, None] == rows[None, None, :]).astype(
        jnp.bfloat16
    )
    outgoing = jnp.einsum("ecr,rd->ecd", pick, normed, preferred_element_type=jnp.float32).astype(
        jnp.bfloat16
    )
    joined = lax.all_to_all(outgoing, "exp", split_axis=0, concat_axis=0, tiled=True)
    gate_part = jnp.einsum(
        "scd,df->scf", joined, expert_gate[0], preferred_element_type=jnp.float32
    )
    up_part = jnp.einsum("scd,df->scf", joined, expert_up[0], preferred_element_type=jnp.float32)
    hidden = (jax.nn.silu(gate_part) * up_part).astype(jnp.bfloat16)
    hidden = lax.optimization_barrier(hidden)
    result = jnp.einsum(
        "scf,fd->scd", hidden, expert_down[0], preferred_element_type=jnp.float32
    ).astype(jnp.bfloat16)
    returned = lax.all_to_all(result, "exp", split_axis=0, concat_axis=0, tiled=True)
    slot_weight = (
        jnp.zeros((experts * capacity,), jnp.float32).at[slot].set(gate_weights.reshape(-1))
    )
    combine = jnp.where(
        table.reshape(experts, capacity)[None, :, :] == rows[:, None, None],
        slot_weight.reshape(experts, capacity)[None, :, :],
        0.0,
    )
    routed = jnp.einsum(
        "rec,ecd->rd",
        combine,
        returned.astype(jnp.float32),
        precision=lax.Precision.HIGHEST,
        preferred_element_type=jnp.float32,
    )
    group_rows = lax.all_gather(normed, "req", axis=0, tiled=True)
    s_gate = jnp.dot(group_rows, shared_gate, preferred_element_type=jnp.float32)
    s_up = jnp.dot(group_rows, shared_up, preferred_element_type=jnp.float32)
    s_hidden = (jax.nn.silu(s_gate) * s_up).astype(jnp.bfloat16)
    s_partial = lax.dot_general(
        s_hidden, shared_down, (((1,), (1,)), ((), ())), preferred_element_type=jnp.float32
    )
    shared = lax.psum_scatter(s_partial, "req", scatter_dimension=0, tiled=True)
    return (stream_f + routed + shared).astype(jnp.bfloat16)


def solution(mesh):
    return jax.shard_map(
        body,
        mesh=mesh,
        in_specs=(
            P(("req", "exp"), None),
            P(("req", "exp"), None),
            P("exp", None),
            P(),
            P(("req", "exp"), None),
            P(("req", "exp"), None),
            P("exp", None, None),
            P("exp", None, None),
            P("exp", None, None),
            P(None, "req"),
            P(None, "req"),
            P(None, "req"),
        ),
        out_specs=P(("req", "exp"), None),
        check_vma=False,
    )
```

profile of v0, /device:TPU:8, one launch (start us, length us, event | category | flops | bytes accessed | tf_op | source)
XLA Modules:
  0.0 291.9 jit_solution(8442988998689780267)
XLA Ops:
  6.5 0.0 copy-start
  6.5 0.0 all-gather.3.cloned.1.call-start
  6.5 1.6 constant_dynamic-slice_fusion
  8.1 0.0 all-gather.3.cloned.1.call-update
  8.1 0.8 copy.20
  8.9 0.1 eq.57
  9.1 0.1 eq.53
  9.2 1.4 copy.18
  10.6 1.7 reduce-window.6
  12.3 0.3 slice_reduce_fusion
  12.6 0.7 broadcast_multiply_fusion
  13.3 0.1 copy.19
  13.4 0.1 mul.58
  13.6 0.1 fusion.29
  13.8 3.4 %scatter_custom_fusion = s32[1152]{0:T(1024)S(1)} fusion(s32[768]{0:T(1024)S(1)} %fusion.38, s32[768]{0:T(1024)S(1)} %add_select_fusion, s32[]{:T(128)} %constant.21.clone.1), kind=kCustom, calls=%fused_computation.54 | custom fusion | bytes 4612 | tf_op jit(solution)/shard_map/scatter | solution.py:42
  17.1 0.1 eq.61
  17.2 0.0 copy-start.3
  17.3 64.5 %all-gather.3.cloned.1.call-done = bf16[2048,2048]{1,0:T(8,128)(2,1)} async-done(((bf16[16,2048]{1,0:T(8,128)(2,1)}), bf16[2048,2048]{1,0:T(8,128)(2,1)}) %all-gather.3.cloned.1.call-update) | async-done | bytes 8388624 | tf_op jit(solution)/shard_map/all_gather | solution.py:30
  81.7 5.8 %multiply_reduce_fusion = (f32[128]{0:T(128)S(1)}, f32[128,2048]{0,1:T(8,128)S(1)}) fusion(bf16[2048,2048]{1,0:T(8,128)(2,1)} %all-gather.3.cloned.1.call-done, bf16[128,2048]{1,0:T(8,128)(2,1)} %param.12, bf16[128,2048]{0,1:T(8,128)(2,1)S(1)} %copy.18), kind=kOutput, calls=%fused_computation.22 | convolution fusion | flops 1075314560 | bytes 10486272 | tf_op jit(solution)/shard_map/dot_general | solution.py:28
  87.6 0.0 copy-done.3
  87.6 0.3 multiply_convert_fusion.1
  87.9 0.0 copy-start.2
  88.0 3.9 %convolution_convert_fusion = bf16[32,36,2048]{2,1,0:T(8,128)(2,1)} fusion(bf16[128,2048]{0,1:T(8,128)(2,1)S(1)} %multiply_convert_fusion.1, s32[32,36]{1,0:T(8,128)S(1)} %eq.61), kind=kOutput, calls=%fused_computation.8 | convolution fusion | flops 606486528 | bytes 5247488 | tf_op jit(solution)/shard_map/ecr,rd->ecd/dot_general | solution.py:47
  91.9 0.0 copy-done.2
  91.9 6.3 %all-to-all-start = ((bf16[32,36,2048]{2,1,0:T(8,128)(2,1)}), bf16[32,36,2048]{2,1,0:T(8,128)(2,1)}, u32[]{:S(2)}, u32[]{:S(2)}) async-start(bf16[32,36,2048]{2,1,0:T(8,128)(2,1)} %convolution_convert_fusion), calls=%async_computation | async-start | bytes 10485760 | tf_op jit(solution)/shard_map/all_to_all | solution.py:50
  98.2 0.0 all-gather.5.cloned.1.call-start
  98.2 0.7 all-gather.5.cloned.1.call-update
  98.9 0.2 reduce-scatter.2.cloned.1.call-start
  99.1 36.2 %all-gather.5.cloned.1.call-done = bf16[512,2048]{0,1:T(8,128)(2,1)} async-done(((bf16[128,2048]{0,1:T(8,128)(2,1)}), bf16[512,2048]{0,1:T(8,128)(2,1)}) %all-gather.5.cloned.1.call-update) | async-done | bytes 2097168 | tf_op jit(solution)/shard_map/all_gather | solution.py:76
  135.3 2.9 %fusion.41 = f32[512,352]{0,1:T(8,128)S(1)} fusion(bf16[2048,352]{0,1:T(8,128)(2,1)} %param.21, bf16[512,2048]{0,1:T(8,128)(2,1)} %all-gather.5.cloned.1.call-done), kind=kOutput, calls=%fused_computation.64 | convolution fusion | flops 738197504 | bytes 4259840 | tf_op jit(solution)/shard_map/dot_general | solution.py:77
  138.3 0.0 copy-done
  138.3 6.2 %fusion.15 = f32[512,2048]{0,1:T(8,128)} fusion(bf16[2048,352]{0,1:T(8,128)(2,1)S(1)} %copy-done, bf16[2048,352]{0,1:T(8,128)(2,1)} %param.22, bf16[512,2048]{0,1:T(8,128)(2,1)} %all-gather.5.cloned.1.call-done, f32[512,352]{0,1:T(8,128)S(1)} %fusion.41), kind=kOutput, calls=%fused_computation.20 | convolution fusion | flops 1477476352 | bytes 9895936 | tf_op jit(solution)/shard_map/dot_general | solution.py:80
  144.5 0.0 reduce-scatter.2.cloned.1.call-update
  144.5 23.7 %all-to-all-done = bf16[32,36,2048]{2,1,0:T(8,128)(2,1)} async-done(((bf16[32,36,2048]{2,1,0:T(8,128)(2,1)}), bf16[32,36,2048]{2,1,0:T(8,128)(2,1)}, u32[]{:S(2)}, u32[]{:S(2)}) %all-to-all-start) | async-done | bytes 4718624 | tf_op jit(solution)/shard_map/all_to_all | solution.py:50
  168.3 0.0 slice-start
  168.3 12.2 %fusion.2 = f32[32,36,1408]{2,1,0:T(8,128)S(1)} fusion(bf16[32,36,2048]{2,1,0:T(8,128)(2,1)} %all-to-all-done, bf16[1,2048,1408]{2,1,0:T(8,128)(2,1)} %param.19), kind=kOutput, calls=%fused_computation.5 | convolution fusion | flops 6643777536 | bytes 16973824 | tf_op jit(solution)/shard_map/scd,df->scf/dot_general | solution.py:54
  180.4 0.0 slice-start.1
  180.4 12.8 %multiply_convert_fusion = bf16[32,36,1408]{2,1,0:T(8,128)(2,1)S(1)} fusion(f32[32,36,1408]{2,1,0:T(8,128)S(1)} %fusion.2, bf16[32,36,2048]{2,1,0:T(8,128)(2,1)} %all-to-all-done, bf16[1,2048,1408]{2,1,0:T(8,128)(2,1)} %param.18), kind=kOutput, calls=%fused_computation.2 | convolution fusion | flops 6653509632 | bytes 20217856 | tf_op jit(solution)/shard_map/scd,df->scf/dot_general | solution.py:51
  193.3 0.0 slice-done
  193.3 0.0 slice-done.1
  193.3 10.2 %fusion.5 = bf16[32,36,2048]{2,1,0:T(8,128)(2,1)} fusion(bf16[32,36,1408]{2,1,0:T(8,128)(2,1)S(1)} %multiply_convert_fusion, bf16[1,1408,2048]{2,1,0:T(8,128)(2,1)S(1)} %bitcast.62), kind=kOutput, calls=%fused_computation.9 | convolution fusion | flops 6646136832 | bytes 13729792 | tf_op jit(solution)/shard_map/scf,fd->scd/dot_general | solution.py:57
  203.5 0.0 copy-start.4
  203.5 5.0 %all-to-all-start.1 = ((bf16[32,36,2048]{2,1,0:T(8,128)(2,1)}), bf16[32,36,2048]{2,1,0:T(8,128)(2,1)}, u32[]{:S(2)}, u32[]{:S(2)}) async-start(bf16[32,36,2048]{2,1,0:T(8,128)(2,1)} %fusion.5), calls=%async_computation.1 | async-start | bytes 10485760 | tf_op jit(solution)/shard_map/all_to_all | solution.py:60
  208.5 0.0 copy-done.4
  208.6 0.0 copy-start.1
  208.6 0.1 copy.23
  208.7 0.1 reshape.80
  208.8 3.4 %scatter_custom_fusion.1 = f32[1152]{0:T(1024)S(1)} fusion(s32[768]{0:T(1024)S(1)} %fusion.38, f32[768]{0:T(1024)S(1)} %reshape.80, f32[]{:T(128)} %constant.44.clone.1), kind=kCustom, calls=%fused_computation.52 | custom fusion | bytes 4612 | tf_op jit(solution)/shard_map/scatter | solution.py:62
  212.2 0.1 broadcast_in_dim.29
  212.3 63.3 %all-to-all-done.1 = bf16[32,36,2048]{2,1,0:T(8,128)(2,1)} async-done(((bf16[32,36,2048]{2,1,0:T(8,128)(2,1)}), bf16[32,36,2048]{2,1,0:T(8,128)(2,1)}, u32[]{:S(2)}, u32[]{:S(2)}) %all-to-all-start.1) | async-done | bytes 4718624 | tf_op jit(solution)/shard_map/all_to_all | solution.py:60
  275.6 0.0 reduce-scatter.2.cloned.1.call-done
  275.6 8.7 %fusion.11 = bf16[128,2048]{0,1:T(8,128)(2,1)S(1)} fusion(f32[128,2048]{0,1:T(8,128)} %reduce-scatter.2.cloned.1.call-done, f32[128,2048]{0,1:T(8,128)S(1)} %get-tuple-element.6, bf16[32,36,2048]{2,1,0:T(8,128)(2,1)} %all-to-all-done.1, f32[32,36]{1,0:T(8,128)S(1)} %broadcast_in_dim.29, s32[32,36]{1,0:T(8,128)S(1)} %eq.61), kind=kOutput, calls=%fused_computation.15 | convolution fusion | flops 3624960000 | bytes 7349248 | tf_op jit(solution)/shard_map/rec,ecd->rd/dot_general | solution.py:69
  284.4 1.0 copy.27
  285.4 0.0 copy-done.1
  (7 shorter events, 0.1 us)
Async XLA Ops:
  6.5 131.7 %copy-start = (bf16[2048,352]{0,1:T(8,128)(2,1)S(1)}, bf16[2048,352]{0,1:T(8,128)(2,1)}, u32[]{:S(2)}) copy-start(bf16[2048,352]{0,1:T(8,128)(2,1)} %param.23) | copy-start | bytes 4325380
  6.5 75.2 %all-gather.3.cloned.1.call-start = ((), (), s32[]{:S(2)}) async-start(), calls=%async_computation.3 | async-start | bytes 8454144 | tf_op jit(solution)/shard_map/all_gather | solution.py:30
  17.2 70.3 %copy-start.3 = (f32[2048]{0:T(1024)S(1)}, f32[2048]{0:T(1024)}, u32[]{:S(2)}) copy-start(f32[2048]{0:T(1024)} %param.15) | copy-start | bytes 24580
  87.9 3.9 %copy-start.2 = (bf16[128,2048]{0,1:T(8,128)(2,1)}, bf16[128,2048]{0,1:T(8,128)(2,1)S(1)}, u32[]{:S(2)}) copy-start(bf16[128,2048]{0,1:T(8,128)(2,1)S(1)} %multiply_convert_fusion.1) | copy-start | bytes 1572868
  91.9 76.4 %all-to-all-start = ((bf16[32,36,2048]{2,1,0:T(8,128)(2,1)}), bf16[32,36,2048]{2,1,0:T(8,128)(2,1)}, u32[]{:S(2)}, u32[]{:S(2)}) async-start(bf16[32,36,2048]{2,1,0:T(8,128)(2,1)} %convolution_convert_fusion), calls=%async_computation | async-start | bytes 10485760 | tf_op jit(solution)/shard_map/all_to_all | solution.py:50
  98.2 37.2 %all-gather.5.cloned.1.call-start = ((), (), s32[]{:S(2)}) async-start(), calls=%async_computation.4 | async-start | bytes 2621440 | tf_op jit(solution)/shard_map/all_gather | solution.py:76
  98.9 176.7 %reduce-scatter.2.cloned.1.call-start = ((), (), s32[]{:S(2)}) async-start(), calls=%async_computation.5 | async-start | bytes 5242880 | tf_op jit(solution)/shard_map/reduce_scatter | solution.py:83
  168.3 25.0 %slice-start = ((s8[5767168]{0:T(1024)(128)(4,1)}), s8[4194304]{0:T(1024)(128)(4,1)S(1)}, s32[]{:S(2)}) async-start(s8[5767168]{0:T(1024)(128)(4,1)} %bitcast.61), calls=%async_computation.6 | async-start | bytes 8388608
  180.4 12.9 %slice-start.1 = ((s8[5767168]{0:T(1024)(128)(4,1)}), s8[1572864]{0:T(1024)(128)(4,1)S(1)}, s32[]{:S(2)}) async-start(s8[5767168]{0:T(1024)(128)(4,1)} %bitcast.61), calls=%async_computation.7 | async-start | bytes 3145728
  203.5 5.0 %copy-start.4 = (f32[128,6]{0,1:T(8,128)S(1)}, f32[128,6]{0,1:T(8,128)}, u32[]{:S(2)}) copy-start(f32[128,6]{0,1:T(8,128)} %param.17) | copy-start | bytes 9220
  203.5 72.1 %all-to-all-start.1 = ((bf16[32,36,2048]{2,1,0:T(8,128)(2,1)}), bf16[32,36,2048]{2,1,0:T(8,128)(2,1)}, u32[]{:S(2)}, u32[]{:S(2)}) async-start(bf16[32,36,2048]{2,1,0:T(8,128)(2,1)} %fusion.5), calls=%async_computation.1 | async-start | bytes 10485760 | tf_op jit(solution)/shard_map/all_to_all | solution.py:60
  208.6 76.8 %copy-start.1 = (bf16[2048,352]{0,1:T(8,128)(2,1)S(1)}, bf16[2048,352]{0,1:T(8,128)(2,1)}, u32[]{:S(2)}) copy-start(bf16[2048,352]{0,1:T(8,128)(2,1)} %param.23) | copy-start | bytes 4325380
Sparse Core Ops, SparseCore 0:
  10.5 71.1 all-gather.2
  100.7 34.6 all-gather.4
  144.7 47.8 reduce-scatter.1
where the time goes:
time: 292 us
  waiting for transfers between devices  188 us (64%)
  matrix products  62.9 us (22%)
  between operations  13.3 us (5%)
  local copies, waits for them, and re-layouts  12.8 us (4%)
  starting transfers between devices  11.5 us (4%)
  other arithmetic  2.96 us (1%)
    all_gather x1, waiting for transfers between devices, body(): lax.all_gather(piece, ('exp', 'req'), axis=0, tiled=True)  64.5 us
    all_to_all x1, waiting for transfers between devices, body(): lax.all_to_all(result, 'exp', split_axis=0, concat_axis=0, tiled=True)  63.3 us
    all_gather x1, waiting for transfers between devices, body(): group_rows = lax.all_gather(normed, 'req', axis=0, tiled=True)  36.2 us
    all_to_all x1, waiting for transfers between devices, body(): lax.all_to_all(outgoing, 'exp', split_axis=0, concat_axis=0, tiled=True)  23.7 us
    dot_general x1, matrix products, body(): jnp.einsum('scd,df->scf', joined, expert_gate[0], preferred_element_type=...  12.8 us
    dot_general x1, matrix products, body(): jnp.einsum('scd,df->scf', joined, expert_up[0], preferred_element_type=jn...  12.2 us
    dot_general x1, matrix products, body(): jnp.einsum('scf,fd->scd', hidden, expert_down[0], preferred_element_type=...  10.2 us
    dot_general x1, matrix products, body(): jnp.einsum('rec,ecd->rd', combine, returned.astype(jnp.float32), precisio...  8.73 us
  transfers between devices with their start and end apart: 5, of which 4 were waited for; matrix products, arithmetic and copies ran while one was open for 20% of the time, Pallas kernels for 0%

commit v1 on v0

--- a/solution.py
+++ b/solution.py
@@ -2,6 +2,7 @@
 import jax.numpy as jnp
 from jax import lax
 from jax.sharding import PartitionSpec as P
+from jax.lax import all_to_all, axis_size
 
 
 def body(
@@ -73,7 +74,13 @@
         precision=lax.Precision.HIGHEST,
         preferred_element_type=jnp.float32,
     )
-    group_rows = lax.all_gather(normed, "req", axis=0, tiled=True)
+
+    def press_the_links(point):
+        return jnp.concatenate(
+            all_to_all(jnp.stack([point for _ in range(axis_size("req"))]), "req", 0, 0), axis=0
+        )
+
+    group_rows = press_the_links(normed)
     s_gate = jnp.dot(group_rows, shared_gate, preferred_element_type=jnp.float32)
     s_up = jnp.dot(group_rows, shared_up, preferred_element_type=jnp.float32)
     s_hidden = (jax.nn.silu(s_gate) * s_up).astype(jnp.bfloat16)

time: 292 us -> 323 us (1.11)
  waiting for transfers between devices: 188 us -> 213 us
  starting transfers between devices: 11.5 us -> 16 us
    all_gather x1 -> x0, waiting for transfers between devices: 36.2 us -> none  [body(): group_rows = lax.all_gather(normed, 'req', axis=0, tiled=True)]
    all_to_all x1, waiting for transfers between devices: 23.7 us -> 59.6 us  [body(): lax.all_to_all(outgoing, 'exp', split_axis=0, concat_axis=0, tiled=True)]
    all_to_all x0 -> x1, waiting for transfers between devices: none -> 16.8 us  [press_the_links(): all_to_all(jnp.stack([point for _ in range(axis_size('req'))]), 'req', 0, 0)]
    all_gather x1, waiting for transfers between devices: 64.5 us -> 72.2 us  [body(): lax.all_gather(piece, ('exp', 'req'), axis=0, tiled=True)]
    all_to_all x0 -> x1, starting transfers between devices: none -> 4.47 us  [press_the_links(): all_to_all(jnp.stack([point for _ in range(axis_size('req'))]), 'req', 0, 0)]
  transfers between devices with their start and end apart: 5 -> 5, of which waited for: 4 -> 4; matrix products, arithmetic and copies ran while one was open for 20% -> 19% of each run, Pallas kernels for 0% -> 0%
where the time goes in v1:
time: 323 us
  waiting for transfers between devices  213 us (66%)
  matrix products  63.8 us (20%)
  starting transfers between devices  16 us (5%)
  local copies, waits for them, and re-layouts  13.9 us (4%)
  between operations  13.6 us (4%)
    all_gather x1, waiting for transfers between devices, body(): lax.all_gather(piece, ('exp', 'req'), axis=0, tiled=True)  72.2 us
    all_to_all x1, waiting for transfers between devices, body(): lax.all_to_all(result, 'exp', split_axis=0, concat_axis=0, tiled=True)  64.5 us
    all_to_all x1, waiting for transfers between devices, body(): lax.all_to_all(outgoing, 'exp', split_axis=0, concat_axis=0, tiled=True)  59.6 us
    all_to_all x1, waiting for transfers between devices, press_the_links(): all_to_all(jnp.stack([point for _ in range(axis_size('req'))]), 'req', 0, 0)  16.8 us
    dot_general x1, matrix products, body(): jnp.einsum('scd,df->scf', joined, expert_gate[0], preferred_element_type=...  12.8 us
    dot_general x1, matrix products, body(): jnp.einsum('scd,df->scf', joined, expert_up[0], preferred_element_type=jn...  12.1 us
    dot_general x1, matrix products, body(): jnp.einsum('scf,fd->scd', hidden, expert_down[0], preferred_element_type=...  10.2 us
    dot_general x1, matrix products, body(): jnp.einsum('rec,ecd->rd', combine, returned.astype(jnp.float32), precisio...  8.73 us
  transfers between devices with their start and end apart: 5, of which 4 were waited for; matrix products, arithmetic and copies ran while one was open for 19% of the time, Pallas kernels for 0%

profile of v1, /device:TPU:8, one launch (start us, length us, event | category | flops | bytes accessed | tf_op | source)
XLA Modules:
  0.0 322.8 jit_solution(7716718514236121637)
XLA Ops:
  6.5 0.0 copy-start
  6.5 0.0 all-gather.2.cloned.1.call-start
  6.5 1.6 constant_dynamic-slice_fusion
  8.1 0.0 all-gather.2.cloned.1.call-update
  8.1 1.3 copy.19
  9.5 0.0 copy-start.3
  9.5 72.2 %all-gather.2.cloned.1.call-done = bf16[2048,2048]{1,0:T(8,128)(2,1)} async-done(((bf16[16,2048]{1,0:T(8,128)(2,1)}), bf16[2048,2048]{1,0:T(8,128)(2,1)}) %all-gather.2.cloned.1.call-update) | async-done | bytes 8388624 | tf_op jit(solution)/shard_map/all_gather | solution.py:31
  81.7 5.8 %multiply_reduce_fusion = (f32[128]{0:T(128)S(1)}, f32[128,2048]{0,1:T(8,128)S(1)}) fusion(bf16[2048,2048]{1,0:T(8,128)(2,1)} %all-gather.2.cloned.1.call-done, bf16[128,2048]{1,0:T(8,128)(2,1)} %param.12, bf16[128,2048]{0,1:T(8,128)(2,1)S(1)} %copy.19), kind=kOutput, calls=%fused_computation.22 | convolution fusion | flops 1075314560 | bytes 10486272 | tf_op jit(solution)/shard_map/dot_general | solution.py:29
  87.5 0.0 copy-start.2
  87.6 0.0 copy-done.3
  87.6 0.3 multiply_convert_fusion.1
  87.9 0.2 copy.27
  88.1 1.6 stack.2
  89.8 4.5 %all-to-all-start.2 = ((bf16[4,128,2048]{2,1,0:T(8,128)(2,1)}), bf16[4,128,2048]{2,1,0:T(8,128)(2,1)}, u32[]{:S(2)}, u32[]{:S(2)}) async-start(bf16[4,128,2048]{2,1,0:T(8,128)(2,1)} %stack.2), calls=%async_computation.2 | async-start | bytes 4194304 | tf_op jit(solution)/shard_map/all_to_all | solution.py:80
  94.2 0.0 copy-done.2
  94.3 0.1 copy.21
  94.4 0.1 eq.57
  94.5 0.1 eq.53
  94.7 1.7 reduce-window.6
  96.4 0.3 slice_reduce_fusion
  96.7 0.1 copy.20
  96.8 0.1 mul.58
  97.0 0.1 fusion.29
  97.1 3.4 %scatter_custom_fusion = s32[1152]{0:T(1024)S(1)} fusion(s32[768]{0:T(1024)S(1)} %fusion.38, s32[768]{0:T(1024)S(1)} %add_select_fusion, s32[]{:T(128)} %constant.21.clone.1), kind=kCustom, calls=%fused_computation.54 | custom fusion | bytes 4612 | tf_op jit(solution)/shard_map/scatter | solution.py:43
  100.5 0.1 eq.61
  100.6 3.9 %convolution_convert_fusion = bf16[32,36,2048]{2,1,0:T(8,128)(2,1)} fusion(bf16[128,2048]{0,1:T(8,128)(2,1)S(1)} %multiply_convert_fusion.1, s32[32,36]{1,0:T(8,128)S(1)} %eq.61), kind=kOutput, calls=%fused_computation.8 | convolution fusion | flops 606486528 | bytes 5247488 | tf_op jit(solution)/shard_map/ecr,rd->ecd/dot_general | solution.py:48
  104.5 16.8 %all-to-all-done.2 = bf16[4,128,2048]{2,1,0:T(8,128)(2,1)} async-done(((bf16[4,128,2048]{2,1,0:T(8,128)(2,1)}), bf16[4,128,2048]{2,1,0:T(8,128)(2,1)}, u32[]{:S(2)}, u32[]{:S(2)}) %all-to-all-start.2) | async-done | bytes 2097184 | tf_op jit(solution)/shard_map/all_to_all | solution.py:80
  121.3 6.3 %all-to-all-start = ((bf16[32,36,2048]{2,1,0:T(8,128)(2,1)}), bf16[32,36,2048]{2,1,0:T(8,128)(2,1)}, u32[]{:S(2)}, u32[]{:S(2)}) async-start(bf16[32,36,2048]{2,1,0:T(8,128)(2,1)} %convolution_convert_fusion), calls=%async_computation | async-start | bytes 10485760 | tf_op jit(solution)/shard_map/all_to_all | solution.py:51
  127.6 0.2 reduce-scatter.2.cloned.1.call-start
  127.8 3.8 %fusion.41 = f32[512,352]{0,1:T(8,128)} fusion(bf16[512,2048]{1,0:T(8,128)(2,1)} %bitcast.10, bf16[2048,352]{0,1:T(8,128)(2,1)} %param.21), kind=kOutput, calls=%fused_computation.64 | convolution fusion | flops 738197504 | bytes 4259840 | tf_op jit(solution)/shard_map/dot_general | solution.py:84
  131.6 0.0 copy-done
  131.6 6.4 %fusion.15 = f32[512,2048]{0,1:T(8,128)} fusion(bf16[2048,352]{0,1:T(8,128)(2,1)S(1)} %copy-done, bf16[512,2048]{1,0:T(8,128)(2,1)} %bitcast.10, bf16[2048,352]{0,1:T(8,128)(2,1)} %param.22, f32[512,352]{0,1:T(8,128)} %fusion.41), kind=kOutput, calls=%fused_computation.20 | convolution fusion | flops 1477476352 | bytes 9895936 | tf_op jit(solution)/shard_map/dot_general | solution.py:87
  138.1 0.0 reduce-scatter.2.cloned.1.call-update
  138.1 59.6 %all-to-all-done = bf16[32,36,2048]{2,1,0:T(8,128)(2,1)} async-done(((bf16[32,36,2048]{2,1,0:T(8,128)(2,1)}), bf16[32,36,2048]{2,1,0:T(8,128)(2,1)}, u32[]{:S(2)}, u32[]{:S(2)}) %all-to-all-start) | async-done | bytes 4718624 | tf_op jit(solution)/shard_map/all_to_all | solution.py:51
  197.7 0.0 slice-start
  197.7 12.1 %fusion.2 = f32[32,36,1408]{2,1,0:T(8,128)S(1)} fusion(bf16[32,36,2048]{2,1,0:T(8,128)(2,1)} %all-to-all-done, bf16[1,2048,1408]{2,1,0:T(8,128)(2,1)} %param.19), kind=kOutput, calls=%fused_computation.5 | convolution fusion | flops 6643777536 | bytes 16973824 | tf_op jit(solution)/shard_map/scd,df->scf/dot_general | solution.py:55
  209.8 0.0 slice-start.1
  209.8 12.8 %multiply_convert_fusion = bf16[32,36,1408]{2,1,0:T(8,128)(2,1)S(1)} fusion(f32[32,36,1408]{2,1,0:T(8,128)S(1)} %fusion.2, bf16[32,36,2048]{2,1,0:T(8,128)(2,1)} %all-to-all-done, bf16[1,2048,1408]{2,1,0:T(8,128)(2,1)} %param.18), kind=kOutput, calls=%fused_computation.2 | convolution fusion | flops 6653509632 | bytes 20217856 | tf_op jit(solution)/shard_map/scd,df->scf/dot_general | solution.py:52
  222.6 0.0 slice-done
  222.7 0.0 slice-done.1
  222.7 10.2 %fusion.5 = bf16[32,36,2048]{2,1,0:T(8,128)(2,1)} fusion(bf16[32,36,1408]{2,1,0:T(8,128)(2,1)S(1)} %multiply_convert_fusion, bf16[1,1408,2048]{2,1,0:T(8,128)(2,1)S(1)} %bitcast.63), kind=kOutput, calls=%fused_computation.9 | convolution fusion | flops 6646136832 | bytes 13729792 | tf_op jit(solution)/shard_map/scf,fd->scd/dot_general | solution.py:58
  232.9 0.0 copy-start.4
  232.9 5.0 %all-to-all-start.1 = ((bf16[32,36,2048]{2,1,0:T(8,128)(2,1)}), bf16[32,36,2048]{2,1,0:T(8,128)(2,1)}, u32[]{:S(2)}, u32[]{:S(2)}) async-start(bf16[32,36,2048]{2,1,0:T(8,128)(2,1)} %fusion.5), calls=%async_computation.1 | async-start | bytes 10485760 | tf_op jit(solution)/shard_map/all_to_all | solution.py:61
  237.9 0.0 copy-done.4
  237.9 0.0 copy-start.1
  237.9 0.1 copy.24
  238.1 0.1 reshape.86
  238.2 3.4 %scatter_custom_fusion.1 = f32[1152]{0:T(1024)S(1)} fusion(s32[768]{0:T(1024)S(1)} %fusion.38, f32[768]{0:T(1024)S(1)} %reshape.86, f32[]{:T(128)} %constant.44.clone.1), kind=kCustom, calls=%fused_computation.52 | custom fusion | bytes 4612 | tf_op jit(solution)/shard_map/scatter | solution.py:63
  241.6 0.1 broadcast_in_dim.29
  241.7 64.5 %all-to-all-done.1 = bf16[32,36,2048]{2,1,0:T(8,128)(2,1)} async-done(((bf16[32,36,2048]{2,1,0:T(8,128)(2,1)}), bf16[32,36,2048]{2,1,0:T(8,128)(2,1)}, u32[]{:S(2)}, u32[]{:S(2)}) %all-to-all-start.1) | async-done | bytes 4718624 | tf_op jit(solution)/shard_map/all_to_all | solution.py:61
  306.2 0.0 reduce-scatter.2.cloned.1.call-done
  306.2 8.7 %fusion.11 = bf16[128,2048]{0,1:T(8,128)(2,1)S(1)} fusion(f32[128,2048]{0,1:T(8,128)} %reduce-scatter.2.cloned.1.call-done, f32[128,2048]{0,1:T(8,128)S(1)} %get-tuple-element.6, bf16[32,36,2048]{2,1,0:T(8,128)(2,1)} %all-to-all-done.1, f32[32,36]{1,0:T(8,128)S(1)} %broadcast_in_dim.29, s32[32,36]{1,0:T(8,128)S(1)} %eq.61), kind=kOutput, calls=%fused_computation.15 | convolution fusion | flops 3624960000 | bytes 7349248 | tf_op jit(solution)/shard_map/rec,ecd->rd/dot_general | solution.py:70
  315.0 1.0 copy.29
  316.0 0.0 copy-done.1
  (8 shorter events, 0.1 us)
Async XLA Ops:
  6.5 125.1 %copy-start = (bf16[2048,352]{0,1:T(8,128)(2,1)S(1)}, bf16[2048,352]{0,1:T(8,128)(2,1)}, u32[]{:S(2)}) copy-start(bf16[2048,352]{0,1:T(8,128)(2,1)} %param.23) | copy-start | bytes 4325380
  6.5 75.2 %all-gather.2.cloned.1.call-start = ((), (), s32[]{:S(2)}) async-start(), calls=%async_computation.4 | async-start | bytes 8454144 | tf_op jit(solution)/shard_map/all_gather | solution.py:31
  9.5 78.1 %copy-start.3 = (f32[2048]{0:T(1024)S(1)}, f32[2048]{0:T(1024)}, u32[]{:S(2)}) copy-start(f32[2048]{0:T(1024)} %param.15) | copy-start | bytes 24580
  87.5 6.7 %copy-start.2 = (s32[128,6]{0,1:T(8,128)S(1)}, s32[128,6]{0,1:T(8,128)}, u32[]{:S(2)}) copy-start(s32[128,6]{0,1:T(8,128)} %param.16) | copy-start | bytes 9220
  89.8 31.5 %all-to-all-start.2 = ((bf16[4,128,2048]{2,1,0:T(8,128)(2,1)}), bf16[4,128,2048]{2,1,0:T(8,128)(2,1)}, u32[]{:S(2)}, u32[]{:S(2)}) async-start(bf16[4,128,2048]{2,1,0:T(8,128)(2,1)} %stack.2), calls=%async_computation.2 | async-start | bytes 4194304 | tf_op jit(solution)/shard_map/all_to_all | solution.py:80
  121.3 76.4 %all-to-all-start = ((bf16[32,36,2048]{2,1,0:T(8,128)(2,1)}), bf16[32,36,2048]{2,1,0:T(8,128)(2,1)}, u32[]{:S(2)}, u32[]{:S(2)}) async-start(bf16[32,36,2048]{2,1,0:T(8,128)(2,1)} %convolution_convert_fusion), calls=%async_computation | async-start | bytes 10485760 | tf_op jit(solution)/shard_map/all_to_all | solution.py:51
  127.6 178.6 %reduce-scatter.2.cloned.1.call-start = ((), (), s32[]{:S(2)}) async-start(), calls=%async_computation.5 | async-start | bytes 5242880 | tf_op jit(solution)/shard_map/reduce_scatter | solution.py:90
  197.7 24.9 %slice-start = ((s8[5767168]{0:T(1024)(128)(4,1)}), s8[4194304]{0:T(1024)(128)(4,1)S(1)}, s32[]{:S(2)}) async-start(s8[5767168]{0:T(1024)(128)(4,1)} %bitcast.62), calls=%async_computation.6 | async-start | bytes 8388608
  209.8 12.8 %slice-start.1 = ((s8[5767168]{0:T(1024)(128)(4,1)}), s8[1572864]{0:T(1024)(128)(4,1)S(1)}, s32[]{:S(2)}) async-start(s8[5767168]{0:T(1024)(128)(4,1)} %bitcast.62), calls=%async_computation.7 | async-start | bytes 3145728
  232.9 5.0 %copy-start.4 = (f32[128,6]{0,1:T(8,128)S(1)}, f32[128,6]{0,1:T(8,128)}, u32[]{:S(2)}) copy-start(f32[128,6]{0,1:T(8,128)} %param.17) | copy-start | bytes 9220
  232.9 73.3 %all-to-all-start.1 = ((bf16[32,36,2048]{2,1,0:T(8,128)(2,1)}), bf16[32,36,2048]{2,1,0:T(8,128)(2,1)}, u32[]{:S(2)}, u32[]{:S(2)}) async-start(bf16[32,36,2048]{2,1,0:T(8,128)(2,1)} %fusion.5), calls=%async_computation.1 | async-start | bytes 10485760 | tf_op jit(solution)/shard_map/all_to_all | solution.py:61
  237.9 78.0 %copy-start.1 = (bf16[2048,352]{0,1:T(8,128)(2,1)S(1)}, bf16[2048,352]{0,1:T(8,128)(2,1)}, u32[]{:S(2)}) copy-start(bf16[2048,352]{0,1:T(8,128)(2,1)} %param.23) | copy-start | bytes 4325380
Sparse Core Ops, SparseCore 0:
  10.5 71.1 all-gather.1
  138.2 46.4 reduce-scatter.1
